TPU v7x, 256 devices: a whole 4x4x8 slice. The times are simulated.
256 devices in a mesh: seq: 32 (over z, y_lo, core), tp: 8 (over x, y_hi).
Axes of the slice: x: 4, y: 4 (y_hi: 2, y_lo: 2; y = y_hi * 2 + y_lo), z: 8, core: 2. Of those that a mesh axis runs over, the one named last changes fastest.
Arguments:
- grad_out: bfloat16 [8192, 14336], P('seq', 'tp'), may hold values from -6 to 6
- weight: bfloat16 [4096, 14336], P('seq', 'tp'), may hold values from -0.046875 to 0.046875
- saved: bfloat16 [8192, 512], P('seq'), may hold values from -0.125 to 0.125
- first_moment: float32 [512, 14336], P('seq', 'tp'), may hold values from -6 to 6
- second_moment: float32 [512, 14336], P('seq', 'tp'), may hold values from 0.05 to 2
- basis: bfloat16 [4096, 512], P('seq'), may hold values from -0.0625 to 0.0625
- new_basis: bfloat16 [4096, 512], P('seq'), may hold values from -0.09375 to 0.09375
Outputs:
- grad_input: float32 [8192, 4096], P('seq', 'tp')
- first_new: float32 [512, 14336], P('seq', 'tp')
- second_new: float32 [512, 14336], P('seq', 'tp')
- update: float32 [512, 14336], P('seq', 'tp')
All inputs are finite; a program needn't handle non-finite values.
Results may differ from a plain program's by a relative error of at most 0.0003.
Values may be sent and summed in bfloat16 or wider, within the bound.
A program may use at most 128 MiB of HBM per device.

v0:
```python
import jax
import jax.numpy as jnp
from jax import lax
from jax.sharding import PartitionSpec as P


def contract_rows(left, right):
    return lax.dot_general(
        left, right, (((0,), (0,)), ((), ())), preferred_element_type=jnp.float32
    )


def exact_dot(left, right):
    return jnp.dot(left, right, precision=lax.Precision.HIGHEST, preferred_element_type=jnp.float32)


def per_device(grad_out, weight, saved, first_moment, second_moment, basis, new_basis):
    rank_rows = first_moment.shape[0]
    row_start = lax.axis_index("seq") * rank_rows
    partial_input = lax.dot_general(
        grad_out,
        lax.all_gather(weight, "seq", axis=0, tiled=True),
        (((1,), (1,)), ((), ())),
        preferred_element_type=jnp.float32,
    )
    grad_input = lax.psum_scatter(partial_input, "tp", scatter_dimension=1, tiled=True)
    local_intersection = contract_rows(new_basis, basis)
    intersection = lax.psum(local_intersection, "seq")
    gradient = lax.psum_scatter(
        contract_rows(saved, grad_out), "seq", scatter_dimension=0, tiled=True
    )
    full_first, full_second = (
        lax.all_gather(first_moment, "seq", axis=0, tiled=True),
        lax.all_gather(second_moment, "seq", axis=0, tiled=True),
    )
    own_rows = lax.dynamic_slice_in_dim(intersection, row_start, rank_rows, 0)
    first_rot = exact_dot(own_rows, full_first)
    second_rot = exact_dot(own_rows * own_rows, full_second)
    first_new = 0.9 * first_rot + 0.1 * gradient
    second_new = 0.95 * second_rot + 0.05 * gradient * gradient
    update = first_new / (jnp.sqrt(second_new) + 1e-08)
    return (grad_input, first_new, second_new, update)


def solution(mesh):
    return jax.shard_map(
        per_device,
        mesh=mesh,
        in_specs=(
            P("seq", "tp"),
            P("seq", "tp"),
            P("seq", None),
            P("seq", "tp"),
            P("seq", "tp"),
            P("seq", None),
            P("seq", None),
        ),
        out_specs=(P("seq", "tp"), P("seq", "tp"), P("seq", "tp"), P("seq", "tp")),
        check_vma=False,
    )
```

profile of v0, /device:TPU:1, one launch (start us, length us, event | category | flops | bytes accessed | tf_op | source)
XLA Modules:
  0.0 695.4 jit_solution(15503047025166529226)
XLA Ops:
  7.2 0.0 all-gather.4.cloned.1.call-start
  7.2 0.7 all-gather.4.cloned.1.call-update
  7.9 0.0 all-reduce.2.cloned.1.call-start
  8.0 2.2 fusion.8
  10.2 0.0 all-reduce.2.cloned.1.call-update
  10.2 0.0 all-gather.8.cloned.1.call-start
  10.3 0.7 all-gather.8.cloned.1.call-update
  11.0 0.0 reduce-scatter.5.cloned.1.call-start
  11.0 3.5 fusion.9
  14.5 0.0 reduce-scatter.5.cloned.1.call-update
  14.6 0.0 all-gather.6.cloned.1.call-start
  14.6 0.5 all-gather.6.cloned.1.call-update
  15.1 0.0 reduce-scatter.3.cloned.1.call-start
  15.2 88.0 %all-gather.4.cloned.1.call-done = bf16[4096,1792]{1,0:T(8,128)(2,1)} async-done(((bf16[128,1792]{1,0:T(8,128)(2,1)}), bf16[4096,1792]{1,0:T(8,128)(2,1)}) %all-gather.4.cloned.1.call-update) | async-done | bytes 14680080 | tf_op jit(solution)/shard_map/all_gather | solution.py:22
  103.2 16.0 %fusion.7 = f32[256,4096]{1,0:T(8,128)} fusion(bf16[256,1792]{1,0:T(8,128)(2,1)S(1)} %copy-done, bf16[4096,1792]{1,0:T(8,128)(2,1)} %all-gather.4.cloned.1.call-done), kind=kOutput, calls=%fused_computation.11 | convolution fusion | flops 3758096384 | bytes 19791872 | tf_op jit(solution)/shard_map/dot_general | solution.py:20
  119.2 0.0 reduce-scatter.3.cloned.1.call-update
  119.2 216.0 %all-reduce.2.cloned.1.call-done = f32[512,512]{1,0:T(8,128)} async-done(((f32[512,512]{1,0:T(8,128)}), f32[512,512]{1,0:T(8,128)}) %all-reduce.2.cloned.1.call-update) | async-done | bytes 1048592 | tf_op jit(solution)/shard_map/psum | solution.py:28
  335.2 68.7 %all-gather.8.cloned.1.call-done = f32[512,1792]{1,0:T(8,128)} async-done(((f32[16,1792]{1,0:T(8,128)}), f32[512,1792]{1,0:T(8,128)}) %all-gather.8.cloned.1.call-update) | async-done | bytes 3670032 | tf_op jit(solution)/shard_map/all_gather | solution.py:34
  403.9 121.5 %reduce-scatter.5.cloned.1.call-done = f32[16,1792]{1,0:T(8,128)} async-done(((f32[512,1792]{1,0:T(8,128)}), f32[16,1792]{1,0:T(8,128)}) %reduce-scatter.5.cloned.1.call-update) | async-done | bytes 114704 | tf_op jit(solution)/shard_map/reduce_scatter | solution.py:29
  525.5 3.8 fusion
  529.3 0.0 copy-start.2
  529.3 66.2 %all-gather.6.cloned.1.call-done = f32[512,1792]{1,0:T(8,128)} async-done(((f32[16,1792]{1,0:T(8,128)}), f32[512,1792]{1,0:T(8,128)}) %all-gather.6.cloned.1.call-update) | async-done | bytes 3670032 | tf_op jit(solution)/shard_map/all_gather | solution.py:33
  595.6 4.5 add_divide_fusion
  600.1 88.4 %reduce-scatter.3.cloned.1.call-done = f32[256,512]{1,0:T(8,128)} async-done(((f32[256,4096]{1,0:T(8,128)}), f32[256,512]{1,0:T(8,128)}) %reduce-scatter.3.cloned.1.call-update) | async-done | bytes 524304 | tf_op jit(solution)/shard_map/reduce_scatter | solution.py:26
  (5 shorter events, 0.0 us)
Async XLA Ops:
  7.2 3.8 copy-start
  7.2 96.0 %all-gather.4.cloned.1.call-start = ((), (), s32[]{:S(2)}) async-start(), calls=%async_computation.2 | async-start | bytes 15138816 | tf_op jit(solution)/shard_map/all_gather | solution.py:22
  7.9 327.3 %all-reduce.2.cloned.1.call-start = ((), (), s32[]{:S(2)}) async-start(), calls=%async_computation.4 | async-start | bytes 2097152 | tf_op jit(solution)/shard_map/psum | solution.py:28
  10.2 393.7 %all-gather.8.cloned.1.call-start = ((), (), s32[]{:S(2)}) async-start(), calls=%async_computation.7 | async-start | bytes 3784704 | tf_op jit(solution)/shard_map/all_gather | solution.py:34
  11.0 514.5 %reduce-scatter.5.cloned.1.call-start = ((), (), s32[]{:S(2)}) async-start(), calls=%async_computation.6 | async-start | bytes 3784704 | tf_op jit(solution)/shard_map/reduce_scatter | solution.py:29
  14.6 581.0 %all-gather.6.cloned.1.call-start = ((), (), s32[]{:S(2)}) async-start(), calls=%async_computation.5 | async-start | bytes 3784704 | tf_op jit(solution)/shard_map/all_gather | solution.py:33
  15.1 673.4 %reduce-scatter.3.cloned.1.call-start = ((), (), s32[]{:S(2)}) async-start(), calls=%async_computation.3 | async-start | bytes 4718592 | tf_op jit(solution)/shard_map/reduce_scatter | solution.py:26
  525.5 70.1 %copy-start.1 = (f32[16,1792]{1,0:T(8,128)S(1)}, f32[16,1792]{1,0:T(8,128)}, u32[]{:S(2)}) copy-start(f32[16,1792]{1,0:T(8,128)} %reduce-scatter.5.cloned.1.call-done) | copy-start | bytes 344068
  529.3 159.2 %copy-start.2 = (f32[16,1792]{1,0:T(8,128)}, f32[16,1792]{1,0:T(8,128)S(1)}, u32[]{:S(2)}) copy-start(f32[16,1792]{1,0:T(8,128)S(1)} %fusion) | copy-start | bytes 344068
Sparse Core Ops, SparseCore 0:
  9.8 93.3 all-gather.3
  105.8 229.3 all-reduce.1
  337.1 66.8 all-gather.7
  406.3 119.0 reduce-scatter.4
  527.2 68.3 all-gather.5
  600.2 88.3 reduce-scatter.2
where the time goes:
time: 696 us; the launch traced here: 695 us
  waiting for transfers between devices  651 us (94%)
  matrix products  30.1 us (4%)
  between operations  14.1 us (2%)
    psum x1, waiting for transfers between devices, per_device(): intersection = lax.psum(local_intersection, 'seq')  216 us
    reduce_scatter x1, waiting for transfers between devices, per_device(): lax.psum_scatter(contract_rows(saved, grad_out), 'seq', scatter_dimension...  122 us
    reduce_scatter x1, waiting for transfers between devices, per_device(): lax.psum_scatter(partial_input, 'tp', scatter_dimension=1, tiled=True)  88.4 us
    all_gather x1, waiting for transfers between devices, per_device(): lax.all_gather(weight, 'seq', axis=0, tiled=True)  88 us
    all_gather x1, waiting for transfers between devices, per_device(): lax.all_gather(second_moment, 'seq', axis=0, tiled=True)  68.7 us
    all_gather x1, waiting for transfers between devices, per_device(): lax.all_gather(first_moment, 'seq', axis=0, tiled=True)  66.2 us
    dot_general x1, matrix products, per_device(): lax.dot_general(grad_out, lax.all_gather(weight, 'seq', axis=0, tiled=Tru...  16 us
  transfers between devices with their start and end apart: 6, of which 6 were waited for; matrix products, arithmetic and copies ran while one was open for 4% of the time, Pallas kernels for 0%

commit v1 on v0

v1 whole, which is shorter than its diff:
```python
import jax
import jax.numpy as jnp
from jax import lax
from jax.experimental import pallas as pl
from jax.experimental.pallas import tpu as pltpu
from jax.sharding import PartitionSpec as P

MESH = pl.DeviceIdType.MESH
F32 = jnp.float32
BF16 = jnp.bfloat16
NZ = 8
TOK = 256
COLS = 1792
HALF = COLS // 2
RANK = 512
ROWS = 16
DROWS = 128
WIDE = COLS + RANK


def rem(a, b):
    return lax.rem(a, jnp.int32(b))


def div(a, b):
    return lax.div(a, jnp.int32(b))


def kernel(
    go, w, sv, fm, sm, ba, nb,
    o_gi, o_f, o_s, o_u,
    Gs, Ws, Pp, Xh, X0, Ff, St, Sq, Nt, Nq, Bs, Ms, Z, ZR, I64, RT, Rr,
    loc, g_s, g_r, k_s, k_r, w_s, w_r, m_s, m_r, z_s, z_r, xa_s, xb_s, h_r, x0_r, f_r,
):
    s = lax.axis_index("seq")
    t = lax.axis_index("tp")
    z, k = div(s, 4), rem(s, 4)
    yl, c = div(k, 2), rem(k, 2)
    x, yh = div(t, 2), rem(t, 2)

    def mate(rel):
        if isinstance(rel, int):
            a, b = rel // 2, rel % 2
        else:
            a, b = div(rel, 2), rem(rel, 2)
        return rem(yl + a, 2) * 2 + rem(c + b, 2)

    def group_dev(rel):
        return (z * 4 + mate(rel), t)

    zl = (rem(z + NZ - 1, NZ) * 4 + k, t)
    zr = (rem(z + 1, NZ) * 4 + k, t)
    xl = (s, rem(x + 3, 4) * 2 + yh)
    xr = (s, rem(x + 1, 4) * 2 + yh)

    barrier = pltpu.get_barrier_semaphore()
    partners = [group_dev(1), group_dev(2), group_dev(3), zl, zr, xl, xr]
    partners += [(z * 4 + mate(r), x * 2 + (1 - yh)) for r in range(4)]
    for dev in partners:
        pl.semaphore_signal(barrier, inc=1, device_id=dev, device_id_type=MESH)
    pl.semaphore_wait(barrier, len(partners))

    def remote(src, dst, ss, rs, dev):
        return pltpu.make_async_remote_copy(
            src_ref=src, dst_ref=dst, send_sem=ss, recv_sem=rs, device_id=dev, device_id_type=MESH
        )

    def zslot(d):
        return 0 if d == 0 else (2 * d - 1 if d > 0 else -2 * d)

    def w_copy(way, j, h):
        sign = 1 if way == 0 else -1
        dst = 7 if j == 4 else zslot(sign * j)
        rows = pl.ds(h * 64, 64)
        src = w.at[rows] if j == 1 else Ws.at[zslot(sign * (j - 1)), rows]
        return remote(src, Ws.at[dst, rows], w_s.at[way, j - 1, h], w_r.at[way, j - 1, h],
                      zl if way == 0 else zr)

    def m_copy(way, j, h, arriving=False):
        dist = j if arriving else j - 1
        blk = rem(z + dist, NZ) if way == 0 else rem(z + NZ - dist, NZ)
        rows = pl.ds(pl.multiple_of(blk * 64 + h * 32, 32), 32)
        return remote(Ms.at[rows], Ms.at[rows], m_s.at[way, j - 1, h], m_r.at[way, j - 1, h],
                      zl if way == 0 else zr)

    def g_copy(rel, h):
        rows = pl.ds(h * 128, 128)
        if rel == 3:
            return remote(Gs.at[2, rows], Gs.at[3, rows], g_s.at[2, h], g_r.at[2, h], group_dev(1))
        return remote(go.at[rows], Gs.at[rel, rows], g_s.at[rel - 1, h], g_r.at[rel - 1, h], group_dev(rel))

    def b_copy(rel):
        if rel == 3:
            return remote(Bs.at[2], Bs.at[3], k_s.at[0, 2], k_r.at[0, 2], group_dev(1))
        return remote(ba, Bs.at[rel], k_s.at[0, rel - 1], k_r.at[0, rel - 1], group_dev(rel))

    def sq_copy(rel):
        return remote(St.at[:, mate(rel)], Sq.at[rel], k_s.at[1, rel - 1], k_r.at[1, rel - 1], group_dev(rel))

    def nq_copy(rel):
        return remote(Nt.at[:, mate(rel)], Nq.at[rel], k_s.at[2, rel - 1], k_r.at[2, rel - 1], group_dev(rel))

    own_rows = pl.ds(pl.multiple_of(z * 64 + k * 16, 16), 16)

    def ma_copy(rel, moment):
        half = rem(yl + rel // 2, 2)
        cols = pl.ds(pl.multiple_of(half * HALF, 128), HALF)
        return remote(moment.at[:, cols], Ms.at[own_rows], k_s.at[3, rel - 1], k_r.at[3, rel - 1], group_dev(rel))

    def i_copy(rel):
        return remote(Z.at[z, :, pl.ds(COLS, RANK)], I64.at[k], k_s.at[4, rel - 1], k_r.at[4, rel - 1], group_dev(rel))

    def r_copy(rel):
        rows = pl.ds(pl.multiple_of(mate(rel) * 16, 16), 16)
        return remote(RT.at[rows], Rr.at[c, yl], k_s.at[5, rel - 1], k_r.at[5, rel - 1], group_dev(rel))

    def z_cols(way, j):
        if j == 0:
            return pl.ds(0, WIDE // 2) if way == 1 else pl.ds(WIDE // 2, WIDE // 2)
        return pl.ds(0, WIDE)

    def z_block(way, j):
        dist = 4 - j
        return rem(z + dist, NZ) if way == 1 else rem(z + NZ - dist, NZ)

    def z_copy(way, j):
        cols = z_cols(way, j)
        return remote(Z.at[z_block(way, j), :, cols], ZR.at[way, j, :, cols], z_s.at[way, j], z_r.at[way, j],
                      zl if way == 0 else zr)

    def cp_a(di, rel):
        return remote(Pp.at[di, rel, pl.ds(0, 128)], Xh.at[di, rel], xa_s.at[di, rel], h_r.at[di, rel], xl)

    def cp_b(di, rel):
        return remote(Pp.at[di, rel, pl.ds(128, 128)], Xh.at[di, rel], xb_s.at[di, rel], h_r.at[di, rel], xr)

    def cp_full(side, di, rel):
        return remote(Pp.at[di, rel], X0.at[side, di, rel], xa_s.at[di, rel], x0_r.at[side, di, rel],
                      xl if side == 0 else xr)

    def cp_f(di, rel, zt, ry):
        return remote(Pp.at[di, rel], Ff.at[ry, rel], xa_s.at[di, rel], f_r.at[ry, rel], (z * 4 + mate(rel), zt))

    def where_to(di):
        mag = div(di + 1, 2)
        d = mag * (2 * rem(di, 2) - 1)
        zt = rem(z + d + NZ, NZ)
        role = rem(x - div(zt, 2) + 4, 4)
        return zt, role

    def stage1(di, rel):
        Pp[di, rel] = lax.dot_general(Gs[rel], Ws[di], (((1,), (1,)), ((), ())), preferred_element_type=F32)
        _, role = where_to(di)

        @pl.when(role == 2)
        def _():
            cp_a(di, rel).start()
            cp_b(di, rel).start()

    def stage2(di, rel):
        _, role = where_to(di)

        @pl.when(role == 1)
        def _():
            cp_a(di, rel).wait_recv()
            Pp[di, rel, pl.ds(0, 128)] = Pp[di, rel, pl.ds(0, 128)] + Xh[di, rel]
            cp_full(0, di, rel).start()

        @pl.when(role == 3)
        def _():
            cp_b(di, rel).wait_recv()
            Pp[di, rel, pl.ds(128, 128)] = Pp[di, rel, pl.ds(128, 128)] + Xh[di, rel]
            cp_full(1, di, rel).start()

    def stage3(di, rel):
        zt, role = where_to(di)

        @pl.when(role == 0)
        def _():
            cp_full(0, di, rel).wait_recv()
            cp_full(1, di, rel).wait_recv()
            total = Pp[di, rel] + X0[0, di, rel] + X0[1, di, rel]
            ry = rem(rem(zt, 2) + yh, 2)
            local = ry + rel == 0

            @pl.when(local)
            def _():
                Ff[0, 0] = total

            @pl.when(jnp.logical_not(local))
            def _():
                Pp[di, rel] = total
                cp_f(di, rel, zt, ry).start()

    def drain(di, rel):
        zt, role = where_to(di)
        ry = rem(rem(zt, 2) + yh, 2)

        @pl.when(role == 2)
        def _():
            cp_a(di, rel).wait_send()
            cp_b(di, rel).wait_send()

        @pl.when(rem(role, 2) == 1)
        def _():
            cp_full(0, di, rel).wait_send()

        @pl.when(jnp.logical_and(role == 0, ry + rel > 0))
        def _():
            cp_f(di, rel, zt, ry).wait_send()

    def run(stage, group):
        d0, dn, r0, rn = group

        def step(i, carry):
            stage(d0 + div(i, rn), r0 + rem(i, rn))
            return carry

        lax.fori_loop(jnp.int32(0), jnp.int32(dn * rn), step, jnp.int32(0))

    A0, A1 = (0, 1, 0, 1), (0, 1, 1, 1)
    A, B, C, D, E, F = (0, 1, 0, 2), (1, 2, 0, 2), (3, 2, 0, 2), (0, 5, 2, 2), (5, 2, 0, 4), (7, 1, 0, 4)

    FIRST = {0: 0, 1: 1}

    def w_hop(j, second):
        for way in (0, 1):
            h = 1 - FIRST[way] if second else FIRST[way]
            if j == 4 and second:
                continue
            w_copy(way, j, h).wait_recv()
            if j < 3 or (j == 3 and not second):
                w_copy(way, j + 1, h).start()

    def m_hop(j, second):
        for way in (0, 1):
            h = 1 - FIRST[way] if second else FIRST[way]
            if j == 4 and second:
                continue
            m_copy(way, j, h, arriving=True).wait_recv()
            if j < 3 or (j == 3 and not second):
                m_copy(way, j + 1, h).start()

    def z_step(j):
        for way in (0, 1):
            if j > 0:
                z_copy(way, j - 1).wait_recv()
                cols = z_cols(way, j - 1)
                blk = z_block(way, j)
                Z[blk, :, cols] = Z[blk, :, cols] + ZR[way, j - 1, :, cols]
            if j < 4:
                z_copy(way, j).start()

    for second in (False, True):
        for way in (0, 1):
            w_copy(way, 1, 1 - FIRST[way] if second else FIRST[way]).start()
    for h in (0, 1):
        g_copy(1, h).start()
    for h in (0, 1):
        g_copy(2, h).start()
    own_g = pltpu.make_async_copy(go, Gs.at[0], loc.at[0])
    own_w = pltpu.make_async_copy(w, Ws.at[0], loc.at[1])
    own_b = pltpu.make_async_copy(ba, Bs.at[0], loc.at[2])
    for cp in (own_g, own_w, own_b):
        cp.start()
    own_cols = pl.ds(pl.multiple_of(yl * HALF, 128), HALF)

    @pl.when(c == 0)
    def _():
        pltpu.make_async_copy(fm.at[:, own_cols], Ms.at[own_rows], loc.at[3]).start()

    @pl.when(c == 1)
    def _():
        pltpu.make_async_copy(sm.at[:, own_cols], Ms.at[own_rows], loc.at[3]).start()

    St[...] = jnp.transpose(sv[...].astype(F32)).astype(BF16).reshape(8, 4, 16, TOK)
    Nt[...] = jnp.transpose(nb[...].astype(F32)).astype(BF16).reshape(8, 4, 16, DROWS)
    Sq[0] = St[:, k]
    Nq[0] = Nt[:, k]
    for rel in (1, 2, 3):
        sq_copy(rel).start()
    for rel in (1, 2, 3):
        nq_copy(rel).start()
    for rel in (1, 2):
        b_copy(rel).start()
    for rel in (1, 2, 3):
        other = rem(c + rel % 2, 2)

        @pl.when(other == 0)
        def _(rel=rel):
            ma_copy(rel, fm).start()

        @pl.when(other == 1)
        def _(rel=rel):
            ma_copy(rel, sm).start()

    own_g.wait()
    own_w.wait()
    run(stage1, A0)
    for h in (0, 1):
        g_copy(1, h).wait_recv()
    run(stage1, A1)
    w_hop(1, False)
    w_hop(1, True)
    g_copy(2, 0).wait_recv()
    g_copy(3, 0).start()
    run(stage1, B)
    run(stage2, A)
    w_hop(2, False)
    run(stage3, A)
    w_hop(2, True)
    run(stage1, C)
    run(stage2, B)
    g_copy(2, 1).wait_recv()
    g_copy(3, 1).start()
    b_copy(2).wait_recv()
    b_copy(3).start()
    g_copy(3, 0).wait_recv()
    g_copy(3, 1).wait_recv()
    run(stage1, D)

    for rel in (1, 2, 3):
        sq_copy(rel).wait_recv()

    def grad_tile(i, carry):
        cols = pl.ds(pl.multiple_of(i * 256, 256), 256)
        acc = jnp.zeros((DROWS, 256), F32)
        for rel in range(4):
            acc += jnp.dot(Sq[rel].reshape(DROWS, TOK), Gs[rel, :, cols], preferred_element_type=F32)
        Z[:, :, cols] = acc.reshape(8, 16, 256)
        return carry

    lax.fori_loop(jnp.int32(0), jnp.int32(COLS // 256), grad_tile, jnp.int32(0))
    own_b.wait()
    b_copy(1).wait_recv()
    b_copy(3).wait_recv()
    for rel in (1, 2, 3):
        nq_copy(rel).wait_recv()
    inter = jnp.zeros((DROWS, RANK), F32)
    for rel in range(4):
        inter += jnp.dot(Nq[rel].reshape(DROWS, DROWS), Bs[rel], preferred_element_type=F32)
    Z[:, :, pl.ds(COLS, RANK)] = inter.reshape(8, 16, RANK)

    w_hop(3, False)
    z_step(0)
    run(stage2, C)
    run(stage3, B)
    w_hop(3, True)
    for rel in (1, 2, 3):
        ma_copy(rel, fm).wait_recv()
    pltpu.make_async_copy(fm.at[:, own_cols], Ms.at[own_rows], loc.at[3]).wait()
    for second in (False, True):
        for way in (0, 1):
            m_copy(way, 1, 1 - FIRST[way] if second else FIRST[way]).start()
    run(stage1, E)
    z_step(1)
    run(stage2, D)
    run(stage3, C)
    w_hop(4, False)
    run(stage1, F)
    m_hop(1, False)
    run(stage2, E)
    m_hop(1, True)
    z_step(2)
    run(stage3, D)
    m_hop(2, False)
    run(stage2, F)
    z_step(3)
    m_hop(2, True)
    run(stage3, E)
    m_hop(3, False)
    z_step(4)
    I64[k] = Z[z, :, pl.ds(COLS, RANK)]
    for rel in (1, 2, 3):
        i_copy(rel).start()
    run(stage3, F)
    m_hop(3, True)
    for rel in (1, 2, 3):
        i_copy(rel).wait_recv()
    m_hop(4, False)

    coef = I64[...].reshape(64, RANK)
    coef = jnp.where(c == 0, coef, coef * coef)
    RT[...] = jnp.dot(coef, Ms[...], precision=lax.Precision.HIGHEST, preferred_element_type=F32)
    for rel in (1, 2, 3):
        r_copy(rel).start()
    Rr[c, yl] = RT[pl.ds(pl.multiple_of(k * 16, 16), 16)]

    for ry in (0, 1):
        for rel in range(4):
            if ry + rel > 0:
                remote(Ff.at[ry, rel], Ff.at[ry, rel], f_r.at[ry, rel], f_r.at[ry, rel], xl).wait_recv()
    for rel in range(4):
        o_gi[:, pl.ds(pl.multiple_of(mate(rel) * 128, 128), 128)] = Ff[0, rel] + Ff[1, rel]

    for rel in (1, 2, 3):
        r_copy(rel).wait_recv()
    for h in (0, 1):
        cols = pl.ds(h * HALF, HALF)
        grad = Z[z, :, cols]
        first = 0.9 * Rr[0, h] + 0.1 * grad
        second = 0.95 * Rr[1, h] + 0.05 * grad * grad
        o_f[:, cols] = first
        o_s[:, cols] = second
        o_u[:, cols] = first / (jnp.sqrt(second) + 1e-8)

    for j in (1, 2, 3, 4):
        for way in (0, 1):
            for h in (0, 1):
                if j < 4 or h == FIRST[way]:
                    w_copy(way, j, h).wait_send()
                    m_copy(way, j, h).wait_send()
    for h in (0, 1):
        for rel in (1, 2, 3):
            g_copy(rel, h).wait_send()
    for rel in (1, 2, 3):
        b_copy(rel).wait_send()
        sq_copy(rel).wait_send()
        nq_copy(rel).wait_send()
        ma_copy(rel, fm).wait_send()
        i_copy(rel).wait_send()
        r_copy(rel).wait_send()
    for j in range(4):
        for way in (0, 1):
            z_copy(way, j).wait_send()
    run(drain, (0, 8, 0, 4))


def per_device(grad_out, weight, saved, first_moment, second_moment, basis, new_basis):
    vmem = pl.BlockSpec(memory_space=pltpu.VMEM)
    dma = pltpu.SemaphoreType.DMA
    rank = jax.ShapeDtypeStruct((ROWS, COLS), F32)
    return pl.pallas_call(
        kernel,
        out_shape=(jax.ShapeDtypeStruct((TOK, RANK), F32), rank, rank, rank),
        in_specs=[vmem] * 7,
        out_specs=(vmem,) * 4,
        scratch_shapes=[
            pltpu.VMEM((4, TOK, COLS), BF16),
            pltpu.VMEM((8, DROWS, COLS), BF16),
            pltpu.VMEM((8, 4, TOK, DROWS), F32),
            pltpu.VMEM((8, 4, DROWS, DROWS), F32),
            pltpu.VMEM((2, 8, 4, TOK, DROWS), F32),
            pltpu.VMEM((2, 4, TOK, DROWS), F32),
            pltpu.VMEM((8, 4, 16, TOK), BF16),
            pltpu.VMEM((4, 8, 16, TOK), BF16),
            pltpu.VMEM((8, 4, 16, DROWS), BF16),
            pltpu.VMEM((4, 8, 16, DROWS), BF16),
            pltpu.VMEM((4, DROWS, RANK), BF16),
            pltpu.VMEM((RANK, HALF), F32),
            pltpu.VMEM((8, 16, WIDE), F32),
            pltpu.VMEM((2, 4, 16, WIDE), F32),
            pltpu.VMEM((4, 16, RANK), F32),
            pltpu.VMEM((64, HALF), F32),
            pltpu.VMEM((2, 2, 16, HALF), F32),
            dma((4,)),
            dma((3, 2)),
            dma((3, 2)),
            dma((6, 3)),
            dma((6, 3)),
            dma((2, 4, 2)),
            dma((2, 4, 2)),
            dma((2, 4, 2)),
            dma((2, 4, 2)),
            dma((2, 4)),
            dma((2, 4)),
            dma((8, 4)),
            dma((8, 4)),
            dma((8, 4)),
            dma((2, 8, 4)),
            dma((2, 4)),
        ],
        compiler_params=pltpu.CompilerParams(
            collective_id=0, has_side_effects=True, vmem_limit_bytes=56 * 1024 * 1024
        ),
    )(grad_out, weight, saved, first_moment, second_moment, basis, new_basis)


def solution(mesh):
    return jax.shard_map(
        per_device,
        mesh=mesh,
        in_specs=(
            P("seq", "tp"),
            P("seq", "tp"),
            P("seq", None),
            P("seq", "tp"),
            P("seq", "tp"),
            P("seq", None),
            P("seq", None),
        ),
        out_specs=(P("seq", "tp"), P("seq", "tp"), P("seq", "tp"), P("seq", "tp")),
        check_vma=False,
    )
```

time: 696 us -> 100 us (0.14)
  waiting for transfers between devices: 651 us -> 0 us
  Pallas kernels: 0 us -> 95.1 us
  matrix products: 30.1 us -> 0 us
  between operations: 14.1 us -> 0.65 us
    all_gather x3 -> x0, waiting for transfers between devices: 223 us -> none  [the longest x1 88 us: per_device(): lax.all_gather(weight, 'seq', axis=0, tiled=True)]
    psum x1 -> x0, waiting for transfers between devices: 216 us -> none  [per_device(): intersection = lax.psum(local_intersection, 'seq')]
    reduce_scatter x2 -> x0, waiting for transfers between devices: 210 us -> none  [the longest x1 122 us: per_device(): lax.psum_scatter(contract_rows(saved, grad_out), 'seq', scatter_dimension...]
    pallas_call x0 -> x1, Pallas kernels: none -> 95.1 us  [per_device(): pl.pallas_call(kernel, out_shape=(jax.ShapeDtypeStruct((TOK, RANK), F32),...]
    dot_general x5 -> x0, matrix products: 30.1 us -> none  [the longest x1 16 us: per_device(): lax.dot_general(grad_out, lax.all_gather(weight, 'seq', axis=0, tiled=Tru...]
  transfers between devices with their start and end apart: 6 -> 0, of which waited for: 6 -> 0; matrix products, arithmetic and copies ran while one was open for 4% -> 0% of each run, Pallas kernels for 0% -> 0%
where the time goes in v1:
time: 100 us
  Pallas kernels  95.1 us (95%)
  local copies, waits for them, and re-layouts  4.43 us (4%)
    pallas_call x1, Pallas kernels, per_device(): pl.pallas_call(kernel, out_shape=(jax.ShapeDtypeStruct((TOK, RANK), F32),...  95.1 us
    unnamed x10, local copies, waits for them, and re-layouts  4.43 us

profile of v1, /device:TPU:1, one launch (start us, length us, event | category | flops | bytes accessed | tf_op | source)
XLA Modules:
  0.0 100.2 jit_solution(12489543985005996017)
XLA Ops:
  0.6 95.1 %shard_map.102 = (f32[256,512]{1,0:T(8,128)}, f32[16,1792]{1,0:T(8,128)}, f32[16,1792]{1,0:T(8,128)}, f32[16,1792]{1,0:T(8,128)}) custom-call(bf16[256,1792]{1,0:T(8,128)(2,1)} %go.1, bf16[128,1792]{1,0:T(8,128)(2,1)} %w.1, bf16[256,512]{1,0:T(8,128)(2,1)} %sv.1, f32[16,1792]{1,0:T(8,128)} %fm.1, f32[16,1792]{1,0:T(8,128)} %sm.1, bf16[128,512]{1,0:T(8,128)(2,1)} %ba.1, ...), custom_call_target="tpu_custom_call" | custom-call | tf_op jit(solution)/shard_map/pallas_call | solution.py:433
  95.8 0.0 copy-start.2
  95.8 1.9 %copy.15 = f32[256,512]{1,0:T(8,128)} copy(f32[256,512]{1,0:T(8,128)} %get-tuple-element.8) | data formatting | bytes 1048576
  97.7 0.0 copy-done.2
  97.7 0.0 copy-start.1
  97.7 0.6 copy.16
  98.3 0.3 copy-done.1
  98.6 0.0 copy-start
  98.6 0.6 copy.17
  99.3 0.3 copy-done
  99.6 0.6 copy.18
Async XLA Ops:
  95.8 1.9 %copy-start.2 = (f32[16,1792]{1,0:T(8,128)S(1)}, f32[16,1792]{1,0:T(8,128)}, u32[]{:S(2)}) copy-start(f32[16,1792]{1,0:T(8,128)} %get-tuple-element.9) | copy-start | bytes 344068
  97.7 0.9 copy-start.1
  98.6 0.9 copy-start

commit v2 on v1

v2 whole, which is shorter than its diff:
```python
import jax
import jax.numpy as jnp
from jax import lax
from jax.experimental import pallas as pl
from jax.experimental.pallas import tpu as pltpu
from jax.sharding import PartitionSpec as P

MESH = pl.DeviceIdType.MESH
F32 = jnp.float32
BF16 = jnp.bfloat16
NZ = 8
TOK = 256
COLS = 1792
HALF = COLS // 2
RANK = 512
ROWS = 16
DROWS = 128


def rem(a, b):
    return lax.rem(a, jnp.int32(b))


def div(a, b):
    return lax.div(a, jnp.int32(b))


def kernel(
    go, w, sv_h, fm, sm, ba, nb_h,
    o_gi, o_f, o_s, o_u,
    sv, nb, Gs, Ws, Pp, Xa, Xb, Ff, St, Sq, Nt, Nq, Bs, Ms, Z, ZR, Y, YR, I64, RT, Rr, gi_v, f_v, s_v, u_v,
    loc, g_s, g_r, k_s, k_r, w_s, w_r, m_s, m_r, z_s, z_r, y_s, y_r, xa_s, xb_s, xa_r, xb_r, f_s, f_r,
):
    s = lax.axis_index("seq")
    t = lax.axis_index("tp")
    z, k = div(s, 4), rem(s, 4)
    yl, c = div(k, 2), rem(k, 2)
    x, yh = div(t, 2), rem(t, 2)

    def mate(rel):
        if isinstance(rel, int):
            a, b = rel // 2, rel % 2
        else:
            a, b = div(rel, 2), rem(rel, 2)
        return rem(yl + a, 2) * 2 + rem(c + b, 2)

    def group_dev(rel):
        return (z * 4 + mate(rel), t)

    zl = (rem(z + NZ - 1, NZ) * 4 + k, t)
    zr = (rem(z + 1, NZ) * 4 + k, t)
    xl = (s, rem(x + 3, 4) * 2 + yh)
    xr = (s, rem(x + 1, 4) * 2 + yh)

    own_rows = pl.ds(pl.multiple_of(z * 64 + k * 16, 16), 16)
    own_cols = pl.ds(pl.multiple_of(yl * HALF, 128), HALF)
    own_g = pltpu.make_async_copy(go, Gs.at[0], loc.at[0])
    own_w = pltpu.make_async_copy(w, Ws.at[0], loc.at[1])
    own_b = pltpu.make_async_copy(ba, Bs.at[0], loc.at[2])
    own_sv = pltpu.make_async_copy(sv_h, sv, loc.at[4])
    own_nb = pltpu.make_async_copy(nb_h, nb, loc.at[5])
    for cp in (own_g, own_w, own_sv, own_nb, own_b):
        cp.start()

    @pl.when(c == 0)
    def _():
        pltpu.make_async_copy(fm.at[:, own_cols], Ms.at[own_rows], loc.at[3]).start()

    @pl.when(c == 1)
    def _():
        pltpu.make_async_copy(sm.at[:, own_cols], Ms.at[own_rows], loc.at[3]).start()

    barrier = pltpu.get_barrier_semaphore()
    partners = [group_dev(1), group_dev(2), group_dev(3), zl, zr, xl, xr]
    partners += [(z * 4 + mate(r), x * 2 + (1 - yh)) for r in range(4)]
    for dev in partners:
        pl.semaphore_signal(barrier, inc=1, device_id=dev, device_id_type=MESH)
    pl.semaphore_wait(barrier, len(partners))

    def remote(src, dst, ss, rs, dev):
        return pltpu.make_async_remote_copy(
            src_ref=src, dst_ref=dst, send_sem=ss, recv_sem=rs, device_id=dev, device_id_type=MESH
        )

    def zslot(d):
        return 0 if d == 0 else (2 * d - 1 if d > 0 else -2 * d)

    def w_copy(way, j, h):
        sign = 1 if way == 0 else -1
        dst = 7 if j == 4 else zslot(sign * j)
        rows = pl.ds(h * 64, 64)
        src = w.at[rows] if j == 1 else Ws.at[zslot(sign * (j - 1)), rows]
        return remote(src, Ws.at[dst, rows], w_s.at[way, j - 1, h], w_r.at[way, j - 1, h],
                      zl if way == 0 else zr)

    def m_copy(way, j, h, arriving=False):
        dist = j if arriving else j - 1
        blk = rem(z + dist, NZ) if way == 0 else rem(z + NZ - dist, NZ)
        rows = pl.ds(pl.multiple_of(blk * 64 + h * 32, 32), 32)
        return remote(Ms.at[rows], Ms.at[rows], m_s.at[way, j - 1, h], m_r.at[way, j - 1, h],
                      zl if way == 0 else zr)

    def g_copy(rel, h):
        rows = pl.ds(h * 128, 128)
        if rel == 3:
            return remote(Gs.at[2, rows], Gs.at[3, rows], g_s.at[2, h], g_r.at[2, h], group_dev(1))
        return remote(go.at[rows], Gs.at[rel, rows], g_s.at[rel - 1, h], g_r.at[rel - 1, h], group_dev(rel))

    def b_copy(rel):
        if rel == 3:
            return remote(Bs.at[2], Bs.at[3], k_s.at[0, 2], k_r.at[0, 2], group_dev(1))
        return remote(ba, Bs.at[rel], k_s.at[0, rel - 1], k_r.at[0, rel - 1], group_dev(rel))

    def sq_copy(rel):
        return remote(St.at[:, mate(rel)], Sq.at[rel], k_s.at[1, rel - 1], k_r.at[1, rel - 1], group_dev(rel))

    def nq_copy(rel):
        return remote(Nt.at[:, mate(rel)], Nq.at[rel], k_s.at[2, rel - 1], k_r.at[2, rel - 1], group_dev(rel))

    def ma_copy(rel, moment):
        half = rem(yl + rel // 2, 2)
        cols = pl.ds(pl.multiple_of(half * HALF, 128), HALF)
        return remote(moment.at[:, cols], Ms.at[own_rows], k_s.at[3, rel - 1], k_r.at[3, rel - 1], group_dev(rel))

    def i_copy(rel):
        return remote(Y.at[z], I64.at[k], k_s.at[4, rel - 1], k_r.at[4, rel - 1], group_dev(rel))

    def r_copy(rel):
        rows = pl.ds(pl.multiple_of(mate(rel) * 16, 16), 16)
        return remote(RT.at[rows], Rr.at[c, yl], k_s.at[5, rel - 1], k_r.at[5, rel - 1], group_dev(rel))

    def z_block(way, j):
        dist = 4 - j
        return rem(z + dist, NZ) if way == 1 else rem(z + NZ - dist, NZ)

    class Tree:
        def __init__(self, own, got, width, ss, rs):
            self.own, self.got, self.width, self.ss, self.rs = own, got, width, ss, rs

        def cols(self, way, j):
            if j == 0:
                return pl.ds((1 - way) * (self.width // 2), self.width // 2)
            return pl.ds(0, self.width)

        def copy(self, way, j):
            cols = self.cols(way, j)
            return remote(self.own.at[z_block(way, j), :, cols], self.got.at[way, j, :, cols],
                          self.ss.at[way, j], self.rs.at[way, j], zl if way == 0 else zr)

        def step(self, j):
            for way in (0, 1):
                if j > 0:
                    self.copy(way, j - 1).wait_recv()
                    cols = self.cols(way, j - 1)
                    blk = z_block(way, j)
                    self.own[blk, :, cols] = self.own[blk, :, cols] + self.got[way, j - 1, :, cols]
                if j < 4:
                    self.copy(way, j).start()

    z_step = Tree(Z, ZR, COLS, z_s, z_r).step
    i_step = Tree(Y, YR, RANK, y_s, y_r).step

    def cp_a(di, rel):
        return remote(Pp.at[di, rel, pl.ds(0, 128)], Xa.at[di, rel], xa_s.at[di], xa_r.at[di, rel], xl)

    def cp_b(di, rel):
        return remote(Pp.at[di, rel, pl.ds(128, 128)], Xb.at[di, rel], xb_s.at[di], xb_r.at[di, rel], xr)

    def cp_f(di, rel, zt, ry):
        return remote(Pp.at[di, rel], Ff.at[ry, rel], f_s.at[ry, rel], f_r.at[ry, rel], (z * 4 + mate(rel), zt))

    def where_to(di):
        mag = div(di + 1, 2)
        d = mag * (2 * rem(di, 2) - 1)
        zt = rem(z + d + NZ, NZ)
        role = rem(x - div(zt, 2) + 4, 4)
        return zt, role

    def take_a(di, rel):
        cp_a(di, rel).wait_recv()
        Pp[di, rel, pl.ds(0, 128)] = Pp[di, rel, pl.ds(0, 128)] + Xa[di, rel]

    def take_b(di, rel):
        cp_b(di, rel).wait_recv()
        Pp[di, rel, pl.ds(128, 128)] = Pp[di, rel, pl.ds(128, 128)] + Xb[di, rel]

    def stage1(di, rel):
        Pp[di, rel] = lax.dot_general(Gs[rel], Ws[di], (((1,), (1,)), ((), ())), preferred_element_type=F32)
        launch(di, rel)

    def stage1_pair(dp, rel):
        di = 2 * dp - 1
        both = Ws[pl.ds(di, 2)].reshape(2 * DROWS, COLS)
        out = lax.dot_general(Gs[rel], both, (((1,), (1,)), ((), ())), preferred_element_type=F32)
        Pp[di, rel] = out[:, :DROWS]
        Pp[di + 1, rel] = out[:, DROWS:]
        launch(di, rel)
        launch(di + 1, rel)

    def launch(di, rel):
        _, role = where_to(di)

        @pl.when(role == 3)
        def _():
            cp_a(di, rel).start()

        @pl.when(role == 1)
        def _():
            cp_b(di, rel).start()

    def stage2(di, rel):
        _, role = where_to(di)

        @pl.when(role == 2)
        def _():
            take_a(di, rel)
            cp_a(di, rel).start()
            take_b(di, rel)
            cp_b(di, rel).start()

    def stage3(di, rel):
        _, role = where_to(di)

        @pl.when(role == 1)
        def _():
            take_a(di, rel)
            cp_a(di, rel).start()

        @pl.when(role == 3)
        def _():
            take_b(di, rel)
            cp_b(di, rel).start()

    def stage4(di, rel):
        zt, role = where_to(di)

        @pl.when(role == 0)
        def _():
            cp_a(di, rel).wait_recv()
            cp_b(di, rel).wait_recv()
            ry = rem(rem(zt, 2) + yh, 2)
            local = ry + rel == 0
            upper = Pp[di, rel, pl.ds(0, 128)] + Xa[di, rel]
            lower = Pp[di, rel, pl.ds(128, 128)] + Xb[di, rel]

            @pl.when(local)
            def _():
                Ff[0, 0, pl.ds(0, 128)] = upper
                Ff[0, 0, pl.ds(128, 128)] = lower

            @pl.when(jnp.logical_not(local))
            def _():
                Pp[di, rel, pl.ds(0, 128)] = upper
                Pp[di, rel, pl.ds(128, 128)] = lower
                cp_f(di, rel, zt, ry).start()

    def drain(di, unused):
        zt, role = where_to(di)
        ry = rem(rem(zt, 2) + yh, 2)

        @pl.when(role > 0)
        def _():
            upper = Pp.at[di, :, pl.ds(0, 128)]
            lower = Pp.at[di, :, pl.ds(128, 128)]
            remote(upper, upper, xa_s.at[di], xa_s.at[di], xl).wait_send()
            remote(lower, lower, xb_s.at[di], xb_s.at[di], xr).wait_send()

        @pl.when(role == 0)
        def _():
            for rel in range(4):
                if rel > 0:
                    cp_f(di, rel, zt, ry).wait_send()
                else:
                    @pl.when(ry > 0)
                    def _():
                        cp_f(di, 0, zt, ry).wait_send()

    def run(stage, group):
        d0, dn, r0, rn = group

        def step(i, carry):
            stage(d0 + div(i, rn), r0 + rem(i, rn))
            return carry

        lax.fori_loop(jnp.int32(0), jnp.int32(dn * rn), step, jnp.int32(0))

    A0, A1 = (0, 1, 0, 1), (0, 1, 1, 1)
    A, B, C, F = (0, 1, 0, 2), (1, 2, 0, 2), (3, 2, 0, 2), (7, 1, 0, 4)
    PB, PC, PD2, PD3, PE = (1, 1, 0, 2), (2, 1, 0, 2), (1, 1, 2, 2), (2, 1, 2, 2), (3, 1, 0, 4)
    D1, D2, D3 = (0, 1, 2, 2), (1, 2, 2, 2), (3, 2, 2, 2)
    E1, E2 = (5 + rem(z + 1, 2), 1, 0, 4), (5 + rem(z, 2), 1, 0, 4)

    FIRST = {0: 0, 1: 1}

    def w_hop(j, second):
        for way in (0, 1):
            h = 1 - FIRST[way] if second else FIRST[way]
            if j == 4 and second:
                continue
            w_copy(way, j, h).wait_recv()
            if j < 3 or (j == 3 and not second):
                w_copy(way, j + 1, h).start()

    def m_hop(j, second):
        for way in (0, 1):
            h = 1 - FIRST[way] if second else FIRST[way]
            if j == 4 and second:
                continue
            m_copy(way, j, h, arriving=True).wait_recv()
            if j < 3 or (j == 3 and not second):
                m_copy(way, j + 1, h).start()

    for second in (False, True):
        for way in (0, 1):
            w_copy(way, 1, 1 - FIRST[way] if second else FIRST[way]).start()
    for rel in (1, 2, 3):
        other = rem(c + rel % 2, 2)

        @pl.when(other == 0)
        def _(rel=rel):
            ma_copy(rel, fm).start()

        @pl.when(other == 1)
        def _(rel=rel):
            ma_copy(rel, sm).start()

    for h in (0, 1):
        g_copy(2, h).start()
    for h in (0, 1):
        g_copy(1, h).start()
    own_g.wait()
    own_w.wait()
    run(stage1, A0)
    for h in (0, 1):
        g_copy(1, h).wait_recv()
    run(stage1, A1)

    own_sv.wait()
    own_nb.wait()
    St[...] = jnp.transpose(sv[...].astype(F32)).astype(BF16).reshape(8, 4, 16, TOK)
    Nt[...] = jnp.transpose(nb[...].astype(F32)).astype(BF16).reshape(8, 4, 16, DROWS)
    Sq[0] = St[:, k]
    Nq[0] = Nt[:, k]
    for rel in (1, 2, 3):
        sq_copy(rel).start()
    for rel in (1, 2):
        b_copy(rel).start()
    for rel in (1, 2, 3):
        nq_copy(rel).start()
    w_hop(1, False)
    run(stage2, A)
    w_hop(1, True)
    run(stage3, A)
    g_copy(2, 0).wait_recv()
    g_copy(3, 0).start()
    run(stage1_pair, PB)
    w_hop(2, False)
    run(stage4, A)
    run(stage2, B)
    w_hop(2, True)
    run(stage1_pair, PC)
    run(stage3, B)
    g_copy(2, 1).wait_recv()
    g_copy(3, 1).start()
    g_copy(3, 0).wait_recv()
    g_copy(3, 1).wait_recv()
    run(stage1, D1)
    w_hop(3, False)
    run(stage1_pair, PD2)
    run(stage1_pair, PD3)
    run(stage2, C)
    b_copy(2).wait_recv()
    b_copy(3).start()

    for rel in (1, 2, 3):
        sq_copy(rel).wait_recv()

    def grad_tile(i, carry):
        cols = pl.ds(pl.multiple_of(i * 256, 256), 256)
        acc = jnp.zeros((DROWS, 256), F32)
        for rel in range(4):
            acc += jnp.dot(Sq[rel].reshape(DROWS, TOK), Gs[rel, :, cols], preferred_element_type=F32)
        Z[:, :, cols] = acc.reshape(8, 16, 256)
        return carry

    lax.fori_loop(jnp.int32(0), jnp.int32(COLS // 256), grad_tile, jnp.int32(0))
    own_b.wait()
    b_copy(1).wait_recv()
    b_copy(3).wait_recv()
    for rel in (1, 2, 3):
        nq_copy(rel).wait_recv()
    inter = jnp.zeros((DROWS, RANK), F32)
    for rel in range(4):
        inter += jnp.dot(Nq[rel].reshape(DROWS, DROWS), Bs[rel], preferred_element_type=F32)
    Y[...] = inter.reshape(8, 16, RANK)
    i_step(0)
    z_step(0)
    for rel in (1, 2, 3):
        ma_copy(rel, fm).wait_recv()
    pltpu.make_async_copy(fm.at[:, own_cols], Ms.at[own_rows], loc.at[3]).wait()
    for second in (False, True):
        for way in (0, 1):
            m_copy(way, 1, 1 - FIRST[way] if second else FIRST[way]).start()
    run(stage2, D1)
    run(stage4, B)
    w_hop(3, True)
    run(stage1_pair, PE)
    run(stage3, C)
    run(stage2, D2)
    run(stage3, D1)
    run(stage2, D3)
    w_hop(4, False)
    run(stage1, F)
    i_step(1)
    z_step(1)
    run(stage2, E1)
    run(stage4, C)
    run(stage3, D2)
    m_hop(1, False)
    run(stage4, D1)
    i_step(2)
    m_hop(1, True)
    run(stage2, F)
    run(stage3, D3)
    run(stage3, E1)
    z_step(2)
    run(stage2, E2)
    m_hop(2, False)
    i_step(3)
    run(stage4, D2)
    run(stage4, D3)
    m_hop(2, True)
    run(stage3, F)
    run(stage4, E1)
    i_step(4)
    I64[k] = Y[z]
    for rel in (1, 2, 3):
        i_copy(rel).start()
    run(stage3, E2)
    z_step(3)
    m_hop(3, False)
    run(stage4, F)
    m_hop(3, True)
    run(stage4, E2)
    run(drain, (0, 5, 0, 1))
    for rel in (1, 2, 3):
        i_copy(rel).wait_recv()
    m_hop(4, False)

    coef = I64[...].reshape(64, RANK)
    coef = jnp.where(c == 0, coef, coef * coef)
    RT[...] = jnp.dot(coef, Ms[...], precision=lax.Precision.HIGHEST, preferred_element_type=F32)
    for rel in (1, 2, 3):
        r_copy(rel).start()
    Rr[c, yl] = RT[pl.ds(pl.multiple_of(k * 16, 16), 16)]

    z_step(4)
    for ry in (0, 1):
        for rel in range(4):
            if ry + rel > 0:
                remote(Ff.at[ry, rel], Ff.at[ry, rel], f_r.at[ry, rel], f_r.at[ry, rel], xl).wait_recv()
    for rel in range(4):
        gi_v[:, pl.ds(pl.multiple_of(mate(rel) * 128, 128), 128)] = Ff[0, rel] + Ff[1, rel]
    out_gi = pltpu.make_async_copy(gi_v, o_gi, loc.at[0])
    out_gi.start()

    for rel in (1, 2, 3):
        r_copy(rel).wait_recv()
    for h in (0, 1):
        cols = pl.ds(h * HALF, HALF)
        grad = Z[z, :, cols]
        first = 0.9 * Rr[0, h] + 0.1 * grad
        second = 0.95 * Rr[1, h] + 0.05 * grad * grad
        f_v[:, cols] = first
        s_v[:, cols] = second
        u_v[:, cols] = first / (jnp.sqrt(second) + 1e-8)

    outs = [out_gi]
    for i, (src, dst) in enumerate(((f_v, o_f), (s_v, o_s), (u_v, o_u))):
        outs.append(pltpu.make_async_copy(src, dst, loc.at[i + 1]))
        outs[-1].start()

    for j in (1, 2, 3, 4):
        for way in (0, 1):
            for h in (0, 1):
                if j < 4 or h == FIRST[way]:
                    w_copy(way, j, h).wait_send()
                    m_copy(way, j, h).wait_send()
    for h in (0, 1):
        for rel in (1, 2, 3):
            g_copy(rel, h).wait_send()
    for rel in (1, 2, 3):
        b_copy(rel).wait_send()
        sq_copy(rel).wait_send()
        nq_copy(rel).wait_send()
        ma_copy(rel, fm).wait_send()
        i_copy(rel).wait_send()
        r_copy(rel).wait_send()
    for j in range(4):
        for way in (0, 1):
            Tree(Z, ZR, COLS, z_s, z_r).copy(way, j).wait_send()
            Tree(Y, YR, RANK, y_s, y_r).copy(way, j).wait_send()
    run(drain, (5, 3, 0, 1))
    for cp in outs:
        cp.wait()


def hand_over(a, b, c, d, oa, ob, oc, od, va, vb, vc, vd, sem):
    triples = ((a, va, oa), (b, vb, ob), (c, vc, oc), (d, vd, od))
    for i, (src, mid, _) in enumerate(triples):
        pltpu.make_async_copy(src, mid, sem.at[0, i]).start()
    for i, (src, mid, dst) in enumerate(triples):
        pltpu.make_async_copy(src, mid, sem.at[0, i]).wait()
        pltpu.make_async_copy(mid, dst, sem.at[1, i]).start()
    for i, (_, mid, dst) in enumerate(triples):
        pltpu.make_async_copy(mid, dst, sem.at[1, i]).wait()


def per_device(grad_out, weight, saved, first_moment, second_moment, basis, new_basis):
    hbm = pl.BlockSpec(memory_space=pl.ANY)
    dma = pltpu.SemaphoreType.DMA
    rank = jax.ShapeDtypeStruct((ROWS, COLS), F32)
    results = pl.pallas_call(
        kernel,
        out_shape=(jax.ShapeDtypeStruct((TOK, RANK), F32), rank, rank, rank),
        in_specs=[hbm] * 7,
        out_specs=(hbm,) * 4,
        scratch_shapes=[
            pltpu.VMEM((TOK, RANK), BF16),
            pltpu.VMEM((DROWS, RANK), BF16),
            pltpu.VMEM((4, TOK, COLS), BF16),
            pltpu.VMEM((8, DROWS, COLS), BF16),
            pltpu.VMEM((8, 4, TOK, DROWS), F32),
            pltpu.VMEM((8, 4, DROWS, DROWS), F32),
            pltpu.VMEM((8, 4, DROWS, DROWS), F32),
            pltpu.VMEM((2, 4, TOK, DROWS), F32),
            pltpu.VMEM((8, 4, 16, TOK), BF16),
            pltpu.VMEM((4, 8, 16, TOK), BF16),
            pltpu.VMEM((8, 4, 16, DROWS), BF16),
            pltpu.VMEM((4, 8, 16, DROWS), BF16),
            pltpu.VMEM((4, DROWS, RANK), BF16),
            pltpu.VMEM((RANK, HALF), F32),
            pltpu.VMEM((8, 16, COLS), F32),
            pltpu.VMEM((2, 4, 16, COLS), F32),
            pltpu.VMEM((8, 16, RANK), F32),
            pltpu.VMEM((2, 4, 16, RANK), F32),
            pltpu.VMEM((4, 16, RANK), F32),
            pltpu.VMEM((64, HALF), F32),
            pltpu.VMEM((2, 2, 16, HALF), F32),
            pltpu.VMEM((TOK, RANK), F32),
            pltpu.VMEM((ROWS, COLS), F32),
            pltpu.VMEM((ROWS, COLS), F32),
            pltpu.VMEM((ROWS, COLS), F32),
            dma((6,)),
            dma((3, 2)),
            dma((3, 2)),
            dma((6, 3)),
            dma((6, 3)),
            dma((2, 4, 2)),
            dma((2, 4, 2)),
            dma((2, 4, 2)),
            dma((2, 4, 2)),
            dma((2, 4)),
            dma((2, 4)),
            dma((2, 4)),
            dma((2, 4)),
            dma((8,)),
            dma((8,)),
            dma((8, 4)),
            dma((8, 4)),
            dma((2, 4)),
            dma((2, 4)),
        ],
        compiler_params=pltpu.CompilerParams(
            collective_id=0, has_side_effects=True, vmem_limit_bytes=56 * 1024 * 1024
        ),
    )(grad_out, weight, saved, first_moment, second_moment, basis, new_basis)
    return pl.pallas_call(
        hand_over,
        out_shape=(jax.ShapeDtypeStruct((TOK, RANK), F32), rank, rank, rank),
        in_specs=[hbm] * 4,
        out_specs=(hbm,) * 4,
        scratch_shapes=[pltpu.VMEM((TOK, RANK), F32)] + [pltpu.VMEM((ROWS, COLS), F32)] * 3 + [dma((2, 4))],
    )(*results)


def solution(mesh):
    return jax.shard_map(
        per_device,
        mesh=mesh,
        in_specs=(
            P("seq", "tp"),
            P("seq", "tp"),
            P("seq", None),
            P("seq", "tp"),
            P("seq", "tp"),
            P("seq", None),
            P("seq", None),
        ),
        out_specs=(P("seq", "tp"), P("seq", "tp"), P("seq", "tp"), P("seq", "tp")),
        check_vma=False,
    )
```

time: 100 us -> 89.9 us (0.90)
  Pallas kernels: 95.1 us -> 89.2 us
  local copies, waits for them, and re-layouts: 4.43 us -> 0 us
    pallas_call x1, Pallas kernels: 95.1 us -> 87.2 us  [per_device(): pl.pallas_call(kernel, out_shape=(jax.ShapeDtypeStruct((TOK, RANK), F32),...]
    unnamed x10 -> x0, local copies, waits for them, and re-layouts: 4.43 us -> none
    pallas_call x0 -> x1, Pallas kernels: none -> 2.01 us  [per_device(): pl.pallas_call(hand_over, out_shape=(jax.ShapeDtypeStruct((TOK, RANK), F3...]
where the time goes in v2:
time: 89.9 us; the launch traced here: 89.8 us
  Pallas kernels  89.2 us (99%)
    pallas_call x1, Pallas kernels, per_device(): pl.pallas_call(kernel, out_shape=(jax.ShapeDtypeStruct((TOK, RANK), F32),...  87.2 us
    pallas_call x1, Pallas kernels, per_device(): pl.pallas_call(hand_over, out_shape=(jax.ShapeDtypeStruct((TOK, RANK), F3...  2.01 us

profile of v2, /device:TPU:1, one launch (start us, length us, event | category | flops | bytes accessed | tf_op | source)
XLA Modules:
  0.0 89.8 jit_solution(7696811556488886116)
XLA Ops:
  0.6 87.2 %shard_map.102 = (f32[256,512]{1,0:T(8,128)}, f32[16,1792]{1,0:T(8,128)}, f32[16,1792]{1,0:T(8,128)}, f32[16,1792]{1,0:T(8,128)}) custom-call(bf16[256,1792]{1,0:T(8,128)(2,1)} %go.1, bf16[128,1792]{1,0:T(8,128)(2,1)} %w.1, bf16[256,512]{1,0:T(8,128)(2,1)} %sv_h.1, f32[16,1792]{1,0:T(8,128)} %fm.1, f32[16,1792]{1,0:T(8,128)} %sm.1, bf16[128,512]{1,0:T(8,128)(2,1)} %ba.1, ...), custom_call_target="tpu_custom_call" | custom-call | tf_op jit(solution)/shard_map/pallas_call | solution.py:523
  87.8 2.0 %shard_map.103 = (f32[256,512]{1,0:T(8,128)}, f32[16,1792]{1,0:T(8,128)}, f32[16,1792]{1,0:T(8,128)}, f32[16,1792]{1,0:T(8,128)}) custom-call(f32[256,512]{1,0:T(8,128)} %get-tuple-element.8.a, f32[16,1792]{1,0:T(8,128)} %get-tuple-element.9.b, f32[16,1792]{1,0:T(8,128)} %get-tuple-element.10.c, f32[16,1792]{1,0:T(8,128)} %get-tuple-element.11.d), custom_call_target="tpu_custom_call" | custom-call | tf_op jit(solution)/shard_map/pallas_call | solution.py:578

commit v3 on v2

--- a/solution.py
+++ b/solution.py
@@ -28,8 +28,8 @@
 def kernel(
     go, w, sv_h, fm, sm, ba, nb_h,
     o_gi, o_f, o_s, o_u,
-    sv, nb, Gs, Ws, Pp, Xa, Xb, Ff, St, Sq, Nt, Nq, Bs, Ms, Z, ZR, Y, YR, I64, RT, Rr, gi_v, f_v, s_v, u_v,
-    loc, g_s, g_r, k_s, k_r, w_s, w_r, m_s, m_r, z_s, z_r, y_s, y_r, xa_s, xb_s, xa_r, xb_r, f_s, f_r,
+    sv, nb, Gs, Ws, Pp, Xa, Xb, Xc, Ff, St, Sq, Nt, Nq, Bs, Ms, Z, ZR, Y, YR, I64, RT, Rr, gi_v, f_v, s_v, u_v,
+    loc, g_s, g_r, k_s, k_r, w_s, w_r, m_s, m_r, z_s, z_r, y_s, y_r, ix_s, ix_r, xa_s, xb_s, xa_r, xb_r, xc_s, xc_r, f_s, f_r,
 ):
     s = lax.axis_index("seq")
     t = lax.axis_index("tp")
@@ -54,9 +54,10 @@
 
     own_rows = pl.ds(pl.multiple_of(z * 64 + k * 16, 16), 16)
     own_cols = pl.ds(pl.multiple_of(yl * HALF, 128), HALF)
+    own_lanes = pl.ds(pl.multiple_of(x * 128, 128), 128)
     own_g = pltpu.make_async_copy(go, Gs.at[0], loc.at[0])
-    own_w = pltpu.make_async_copy(w, Ws.at[0], loc.at[1])
-    own_b = pltpu.make_async_copy(ba, Bs.at[0], loc.at[2])
+    own_w = pltpu.make_async_copy(w, Ws.at[pl.ds(0, DROWS)], loc.at[1])
+    own_b = pltpu.make_async_copy(ba.at[:, own_lanes], Bs.at[0], loc.at[2])
     own_sv = pltpu.make_async_copy(sv_h, sv, loc.at[4])
     own_nb = pltpu.make_async_copy(nb_h, nb, loc.at[5])
     for cp in (own_g, own_w, own_sv, own_nb, own_b):
@@ -72,6 +73,7 @@
 
     barrier = pltpu.get_barrier_semaphore()
     partners = [group_dev(1), group_dev(2), group_dev(3), zl, zr, xl, xr]
+    partners.append((s, rem(x + 2, 4) * 2 + yh))
     partners += [(z * 4 + mate(r), x * 2 + (1 - yh)) for r in range(4)]
     for dev in partners:
         pl.semaphore_signal(barrier, inc=1, device_id=dev, device_id_type=MESH)
@@ -89,82 +91,92 @@
         sign = 1 if way == 0 else -1
         dst = 7 if j == 4 else zslot(sign * j)
         rows = pl.ds(h * 64, 64)
-        src = w.at[rows] if j == 1 else Ws.at[zslot(sign * (j - 1)), rows]
-        return remote(src, Ws.at[dst, rows], w_s.at[way, j - 1, h], w_r.at[way, j - 1, h],
+        src = w.at[rows] if j == 1 else Ws.at[pl.ds(zslot(sign * (j - 1)) * DROWS + h * 64, 64)]
+        return remote(src, Ws.at[pl.ds(dst * DROWS + h * 64, 64)], w_s.at[way], w_r.at[way, j - 1, h],
                       zl if way == 0 else zr)
 
     def m_copy(way, j, h, arriving=False):
         dist = j if arriving else j - 1
         blk = rem(z + dist, NZ) if way == 0 else rem(z + NZ - dist, NZ)
         rows = pl.ds(pl.multiple_of(blk * 64 + h * 32, 32), 32)
-        return remote(Ms.at[rows], Ms.at[rows], m_s.at[way, j - 1, h], m_r.at[way, j - 1, h],
+        return remote(Ms.at[rows], Ms.at[rows], m_s.at[way], m_r.at[way, j - 1, h],
                       zl if way == 0 else zr)
 
     def g_copy(rel, h):
         rows = pl.ds(h * 128, 128)
         if rel == 3:
-            return remote(Gs.at[2, rows], Gs.at[3, rows], g_s.at[2, h], g_r.at[2, h], group_dev(1))
-        return remote(go.at[rows], Gs.at[rel, rows], g_s.at[rel - 1, h], g_r.at[rel - 1, h], group_dev(rel))
+            return remote(Gs.at[2, rows], Gs.at[3, rows], g_s.at[0], g_r.at[2, h], group_dev(1))
+        return remote(go.at[rows], Gs.at[rel, rows], g_s.at[0], g_r.at[rel - 1, h], group_dev(rel))
 
     def b_copy(rel):
         if rel == 3:
-            return remote(Bs.at[2], Bs.at[3], k_s.at[0, 2], k_r.at[0, 2], group_dev(1))
-        return remote(ba, Bs.at[rel], k_s.at[0, rel - 1], k_r.at[0, rel - 1], group_dev(rel))
+            return remote(Bs.at[2], Bs.at[3], k_s.at[0], k_r.at[0, 2], group_dev(1))
+        return remote(ba.at[:, own_lanes], Bs.at[rel], k_s.at[0], k_r.at[0, rel - 1], group_dev(rel))
 
     def sq_copy(rel):
-        return remote(St.at[:, mate(rel)], Sq.at[rel], k_s.at[1, rel - 1], k_r.at[1, rel - 1], group_dev(rel))
+        return remote(St.at[:, mate(rel)], Sq.at[rel], k_s.at[1], k_r.at[1, rel - 1], group_dev(rel))
 
     def nq_copy(rel):
-        return remote(Nt.at[:, mate(rel)], Nq.at[rel], k_s.at[2, rel - 1], k_r.at[2, rel - 1], group_dev(rel))
+        return remote(Nt.at[:, mate(rel)], Nq.at[rel], k_s.at[2], k_r.at[2, rel - 1], group_dev(rel))
 
     def ma_copy(rel, moment):
         half = rem(yl + rel // 2, 2)
         cols = pl.ds(pl.multiple_of(half * HALF, 128), HALF)
-        return remote(moment.at[:, cols], Ms.at[own_rows], k_s.at[3, rel - 1], k_r.at[3, rel - 1], group_dev(rel))
+        return remote(moment.at[:, cols], Ms.at[own_rows], k_s.at[3], k_r.at[3, rel - 1], group_dev(rel))
 
     def i_copy(rel):
-        return remote(Y.at[z], I64.at[k], k_s.at[4, rel - 1], k_r.at[4, rel - 1], group_dev(rel))
+        return remote(I64.at[k], I64.at[k], k_s.at[4], k_r.at[4, rel - 1], group_dev(rel))
+
+    def ix_copy(step):
+        return remote(Y.at[z], I64.at[k, x], ix_s.at[0], ix_r.at[step - 1], (s, rem(x + step, 4) * 2 + yh))
 
     def r_copy(rel):
         rows = pl.ds(pl.multiple_of(mate(rel) * 16, 16), 16)
-        return remote(RT.at[rows], Rr.at[c, yl], k_s.at[5, rel - 1], k_r.at[5, rel - 1], group_dev(rel))
+        return remote(RT.at[rows], Rr.at[c, yl], k_s.at[5], k_r.at[5, rel - 1], group_dev(rel))
 
     def z_block(way, j):
         dist = 4 - j
         return rem(z + dist, NZ) if way == 1 else rem(z + NZ - dist, NZ)
 
     class Tree:
-        def __init__(self, own, got, width, ss, rs):
-            self.own, self.got, self.width, self.ss, self.rs = own, got, width, ss, rs
-
-        def cols(self, way, j):
-            if j == 0:
-                return pl.ds((1 - way) * (self.width // 2), self.width // 2)
-            return pl.ds(0, self.width)
+        def __init__(self, own, got, ss, rs):
+            self.own, self.got, self.ss, self.rs = own, got, ss, rs
+
+        def part(self, way, j):
+            return pl.ds((1 - way) * 8, 8) if j == 0 else pl.ds(0, 16)
 
         def copy(self, way, j):
-            cols = self.cols(way, j)
-            return remote(self.own.at[z_block(way, j), :, cols], self.got.at[way, j, :, cols],
-                          self.ss.at[way, j], self.rs.at[way, j], zl if way == 0 else zr)
+            part = self.part(way, j)
+            return remote(self.own.at[z_block(way, j), part], self.got.at[way, j, part],
+                          self.ss.at[way], self.rs.at[way, j], zl if way == 0 else zr)
 
         def step(self, j):
             for way in (0, 1):
                 if j > 0:
                     self.copy(way, j - 1).wait_recv()
-                    cols = self.cols(way, j - 1)
+                    part = self.part(way, j - 1)
                     blk = z_block(way, j)
-                    self.own[blk, :, cols] = self.own[blk, :, cols] + self.got[way, j - 1, :, cols]
+                    self.own[blk, part] = self.own[blk, part] + self.got[way, j - 1, part]
                 if j < 4:
                     self.copy(way, j).start()
 
-    z_step = Tree(Z, ZR, COLS, z_s, z_r).step
-    i_step = Tree(Y, YR, RANK, y_s, y_r).step
+        def close(self):
+            for way in (0, 1):
+                sent = self.own.at[pl.ds(0, 7), pl.ds(0, 8)]
+                remote(sent, sent, self.ss.at[way], self.ss.at[way], zl).wait_send()
+
+    z_tree, i_tree = Tree(Z, ZR, z_s, z_r), Tree(Y, YR, y_s, y_r)
+    z_step, i_step = z_tree.step, i_tree.step
 
     def cp_a(di, rel):
         return remote(Pp.at[di, rel, pl.ds(0, 128)], Xa.at[di, rel], xa_s.at[di], xa_r.at[di, rel], xl)
 
     def cp_b(di, rel):
         return remote(Pp.at[di, rel, pl.ds(128, 128)], Xb.at[di, rel], xb_s.at[di], xb_r.at[di, rel], xr)
+
+    def cp_c(di, rel):
+        return remote(Pp.at[di, rel], Xc.at[di - 5, rel], xc_s.at[di - 5, rel], xc_r.at[di - 5, rel],
+                      (s, x * 2 + (1 - yh)))
 
     def cp_f(di, rel, zt, ry):
         return remote(Pp.at[di, rel], Ff.at[ry, rel], f_s.at[ry, rel], f_r.at[ry, rel], (z * 4 + mate(rel), zt))
@@ -176,6 +188,20 @@
         role = rem(x - div(zt, 2) + 4, 4)
         return zt, role
 
+    near = 5 + rem(z + 1, 2)
+    far = 5 + rem(z, 2)
+
+    def crossing(di, rel):
+        zt, _ = where_to(di)
+        ry = rem(rem(zt, 2) + yh, 2)
+        early = jnp.logical_and(jnp.logical_or(di == 7, di == near), rel < 2)
+        early = jnp.logical_or(early, jnp.logical_and(di == far, rel < 1))
+        return jnp.logical_and(early, ry == 1), jnp.logical_and(early, ry == 0), early
+
+    def in_ring(di, rel, role_is):
+        away, _, _ = crossing(di, rel)
+        return jnp.logical_and(jnp.logical_not(away), role_is)
+
     def take_a(di, rel):
         cp_a(di, rel).wait_recv()
         Pp[di, rel, pl.ds(0, 128)] = Pp[di, rel, pl.ds(0, 128)] + Xa[di, rel]
@@ -184,13 +210,16 @@
         cp_b(di, rel).wait_recv()
         Pp[di, rel, pl.ds(128, 128)] = Pp[di, rel, pl.ds(128, 128)] + Xb[di, rel]
 
+    def w_rows(di, n):
+        return Ws[pl.ds(pl.multiple_of(di * DROWS, DROWS), n)]
+
     def stage1(di, rel):
-        Pp[di, rel] = lax.dot_general(Gs[rel], Ws[di], (((1,), (1,)), ((), ())), preferred_element_type=F32)
+        Pp[di, rel] = lax.dot_general(Gs[rel], w_rows(di, DROWS), (((1,), (1,)), ((), ())), preferred_element_type=F32)
         launch(di, rel)
 
     def stage1_pair(dp, rel):
         di = 2 * dp - 1
-        both = Ws[pl.ds(di, 2)].reshape(2 * DROWS, COLS)
+        both = w_rows(di, 2 * DROWS)
         out = lax.dot_general(Gs[rel], both, (((1,), (1,)), ((), ())), preferred_element_type=F32)
         Pp[di, rel] = out[:, :DROWS]
         Pp[di + 1, rel] = out[:, DROWS:]
@@ -199,6 +228,18 @@
 
     def launch(di, rel):
         _, role = where_to(di)
+        away, _, early = crossing(di, rel)
+
+        @pl.when(away)
+        def _():
+            cp_c(di, rel).start()
+
+        @pl.when(jnp.logical_not(early))
+        def _():
+            enter(di, rel)
+
+    def enter(di, rel):
+        _, role = where_to(di)
 
         @pl.when(role == 3)
         def _():
@@ -207,11 +248,20 @@
         @pl.when(role == 1)
         def _():
             cp_b(di, rel).start()
+
+    def merge(di, rel):
+        _, home, _ = crossing(di, rel)
+
+        @pl.when(home)
+        def _():
+            cp_c(di, rel).wait_recv()
+            Pp[di, rel] = Pp[di, rel] + Xc[di - 5, rel]
+            enter(di, rel)
 
     def stage2(di, rel):
         _, role = where_to(di)
 
-        @pl.when(role == 2)
+        @pl.when(in_ring(di, rel, role == 2))
         def _():
             take_a(di, rel)
             cp_a(di, rel).start()
@@ -221,12 +271,12 @@
     def stage3(di, rel):
         _, role = where_to(di)
 
-        @pl.when(role == 1)
+        @pl.when(in_ring(di, rel, role == 1))
         def _():
             take_a(di, rel)
             cp_a(di, rel).start()
 
-        @pl.when(role == 3)
+        @pl.when(in_ring(di, rel, role == 3))
         def _():
             take_b(di, rel)
             cp_b(di, rel).start()
@@ -234,7 +284,7 @@
     def stage4(di, rel):
         zt, role = where_to(di)
 
-        @pl.when(role == 0)
+        @pl.when(in_ring(di, rel, role == 0))
         def _():
             cp_a(di, rel).wait_recv()
             cp_b(di, rel).wait_recv()
@@ -257,23 +307,41 @@
     def drain(di, unused):
         zt, role = where_to(di)
         ry = rem(rem(zt, 2) + yh, 2)
-
-        @pl.when(role > 0)
-        def _():
-            upper = Pp.at[di, :, pl.ds(0, 128)]
-            lower = Pp.at[di, :, pl.ds(128, 128)]
-            remote(upper, upper, xa_s.at[di], xa_s.at[di], xl).wait_send()
-            remote(lower, lower, xb_s.at[di], xb_s.at[di], xr).wait_send()
+        away0, _, _ = crossing(di, 0)
+        away1, _, _ = crossing(di, 1)
+
+        def ring_sends(cond, lo, n):
+            @pl.when(jnp.logical_and(role > 0, cond))
+            def _():
+                upper = Pp.at[di, pl.ds(lo, n), pl.ds(0, 128)]
+                lower = Pp.at[di, pl.ds(lo, n), pl.ds(128, 128)]
+                remote(upper, upper, xa_s.at[di], xa_s.at[di], xl).wait_send()
+                remote(lower, lower, xb_s.at[di], xb_s.at[di], xr).wait_send()
+
+        ring_sends(away1, 2, 2)
+        ring_sends(jnp.logical_and(away0, jnp.logical_not(away1)), 1, 3)
+        ring_sends(jnp.logical_not(away0), 0, 4)
+
+        @pl.when(away0)
+        def _():
+            cp_c(di, 0).wait_send()
+
+        @pl.when(away1)
+        def _():
+            cp_c(di, 1).wait_send()
 
         @pl.when(role == 0)
         def _():
-            for rel in range(4):
-                if rel > 0:
-                    cp_f(di, rel, zt, ry).wait_send()
-                else:
-                    @pl.when(ry > 0)
-                    def _():
-                        cp_f(di, 0, zt, ry).wait_send()
+            for rel in (2, 3):
+                cp_f(di, rel, zt, ry).wait_send()
+
+            @pl.when(jnp.logical_not(away1))
+            def _():
+                cp_f(di, 1, zt, ry).wait_send()
+
+            @pl.when(jnp.logical_and(jnp.logical_not(away0), ry > 0))
+            def _():
+                cp_f(di, 0, zt, ry).wait_send()
 
     def run(stage, group):
         d0, dn, r0, rn = group
@@ -288,7 +356,9 @@
     A, B, C, F = (0, 1, 0, 2), (1, 2, 0, 2), (3, 2, 0, 2), (7, 1, 0, 4)
     PB, PC, PD2, PD3, PE = (1, 1, 0, 2), (2, 1, 0, 2), (1, 1, 2, 2), (2, 1, 2, 2), (3, 1, 0, 4)
     D1, D2, D3 = (0, 1, 2, 2), (1, 2, 2, 2), (3, 2, 2, 2)
-    E1, E2 = (5 + rem(z + 1, 2), 1, 0, 4), (5 + rem(z, 2), 1, 0, 4)
+    E1, E2 = (near, 1, 2, 2), (far, 1, 1, 3)
+    G0 = (far, 1, 0, 1)
+    E0, F0, F1 = (near, 1, 0, 2), (7, 1, 0, 2), (7, 1, 2, 2)
 
     FIRST = {0: 0, 1: 1}
 
@@ -324,10 +394,22 @@
         def _(rel=rel):
             ma_copy(rel, sm).start()
 
-    for h in (0, 1):
-        g_copy(2, h).start()
+    g_copy(2, 0).start()
     for h in (0, 1):
         g_copy(1, h).start()
+    own_nb.wait()
+    Nt[...] = jnp.transpose(nb[...].astype(F32)).astype(BF16).reshape(8, 4, 16, DROWS)
+    Nq[0] = Nt[:, k]
+    for rel in (1, 2):
+        b_copy(rel).start()
+    for rel in (1, 2, 3):
+        nq_copy(rel).start()
+    g_copy(2, 1).start()
+    own_sv.wait()
+    St[...] = jnp.transpose(sv[...].astype(F32)).astype(BF16).reshape(8, 4, 16, TOK)
+    Sq[0] = St[:, k]
+    for rel in (1, 2, 3):
+        sq_copy(rel).start()
     own_g.wait()
     own_w.wait()
     run(stage1, A0)
@@ -335,25 +417,25 @@
         g_copy(1, h).wait_recv()
     run(stage1, A1)
 
-    own_sv.wait()
-    own_nb.wait()
-    St[...] = jnp.transpose(sv[...].astype(F32)).astype(BF16).reshape(8, 4, 16, TOK)
-    Nt[...] = jnp.transpose(nb[...].astype(F32)).astype(BF16).reshape(8, 4, 16, DROWS)
-    Sq[0] = St[:, k]
-    Nq[0] = Nt[:, k]
-    for rel in (1, 2, 3):
-        sq_copy(rel).start()
-    for rel in (1, 2):
-        b_copy(rel).start()
-    for rel in (1, 2, 3):
-        nq_copy(rel).start()
     w_hop(1, False)
     run(stage2, A)
     w_hop(1, True)
     run(stage3, A)
     g_copy(2, 0).wait_recv()
     g_copy(3, 0).start()
+    b_copy(2).wait_recv()
+    b_copy(3).start()
     run(stage1_pair, PB)
+    own_b.wait()
+    b_copy(1).wait_recv()
+    b_copy(3).wait_recv()
+    for rel in (1, 2, 3):
+        nq_copy(rel).wait_recv()
+    inter = jnp.zeros((DROWS, 128), F32)
+    for rel in range(4):
+        inter += jnp.dot(Nq[rel].reshape(DROWS, DROWS), Bs[rel], preferred_element_type=F32)
+    Y[...] = inter.reshape(8, 16, 128)
+    i_step(0)
     w_hop(2, False)
     run(stage4, A)
     run(stage2, B)
@@ -368,9 +450,8 @@
     w_hop(3, False)
     run(stage1_pair, PD2)
     run(stage1_pair, PD3)
+    i_step(1)
     run(stage2, C)
-    b_copy(2).wait_recv()
-    b_copy(3).start()
 
     for rel in (1, 2, 3):
         sq_copy(rel).wait_recv()
@@ -384,16 +465,6 @@
         return carry
 
     lax.fori_loop(jnp.int32(0), jnp.int32(COLS // 256), grad_tile, jnp.int32(0))
-    own_b.wait()
-    b_copy(1).wait_recv()
-    b_copy(3).wait_recv()
-    for rel in (1, 2, 3):
-        nq_copy(rel).wait_recv()
-    inter = jnp.zeros((DROWS, RANK), F32)
-    for rel in range(4):
-        inter += jnp.dot(Nq[rel].reshape(DROWS, DROWS), Bs[rel], preferred_element_type=F32)
-    Y[...] = inter.reshape(8, 16, RANK)
-    i_step(0)
     z_step(0)
     for rel in (1, 2, 3):
         ma_copy(rel, fm).wait_recv()
@@ -411,59 +482,92 @@
     run(stage2, D3)
     w_hop(4, False)
     run(stage1, F)
-    i_step(1)
     z_step(1)
+    i_step(2)
     run(stage2, E1)
     run(stage4, C)
+    m_hop(1, False)
+    run(stage2, E2)
     run(stage3, D2)
-    m_hop(1, False)
     run(stage4, D1)
-    i_step(2)
+    i_step(3)
     m_hop(1, True)
-    run(stage2, F)
+    run(stage2, F1)
     run(stage3, D3)
     run(stage3, E1)
     z_step(2)
-    run(stage2, E2)
     m_hop(2, False)
-    i_step(3)
+    i_step(4)
+    I64[k, x] = Y[z]
+    for step in (1, 2, 3):
+        ix_copy(step).start()
     run(stage4, D2)
+    run(merge, E0)
+    run(stage3, F1)
+    m_hop(2, True)
+    run(merge, G0)
+    run(stage3, E2)
     run(stage4, D3)
-    m_hop(2, True)
-    run(stage3, F)
+    run(merge, F0)
+    run(stage2, E0)
+    run(stage2, G0)
     run(stage4, E1)
-    i_step(4)
-    I64[k] = Y[z]
+    m_hop(3, False)
+    z_step(3)
+    for step in (1, 2, 3):
+        ix_copy(step).wait_recv()
     for rel in (1, 2, 3):
         i_copy(rel).start()
-    run(stage3, E2)
-    z_step(3)
-    m_hop(3, False)
-    run(stage4, F)
+    run(stage2, F0)
+    run(stage4, E2)
+    run(stage4, F1)
+    run(stage3, E0)
+    run(stage3, G0)
     m_hop(3, True)
-    run(stage4, E2)
+    run(stage3, F0)
     run(drain, (0, 5, 0, 1))
     for rel in (1, 2, 3):
         i_copy(rel).wait_recv()
     m_hop(4, False)
 
-    coef = I64[...].reshape(64, RANK)
+    coef = jnp.concatenate([I64[:, i].reshape(64, 128) for i in range(4)], axis=1)
     coef = jnp.where(c == 0, coef, coef * coef)
     RT[...] = jnp.dot(coef, Ms[...], precision=lax.Precision.HIGHEST, preferred_element_type=F32)
     for rel in (1, 2, 3):
         r_copy(rel).start()
+    run(stage4, E0)
+    run(stage4, G0)
+    run(stage4, F0)
     Rr[c, yl] = RT[pl.ds(pl.multiple_of(k * 16, 16), 16)]
 
-    z_step(4)
-    for ry in (0, 1):
-        for rel in range(4):
-            if ry + rel > 0:
-                remote(Ff.at[ry, rel], Ff.at[ry, rel], f_r.at[ry, rel], f_r.at[ry, rel], xl).wait_recv()
+    def piece(ry, rel):
+        remote(Ff.at[ry, rel], Ff.at[ry, rel], f_r.at[ry, rel], f_r.at[ry, rel], xl).wait_recv()
+
+    ahead = rem(t - z + NZ, NZ)
+    merged = jnp.logical_or(ahead == 4, ahead == 5 - 2 * rem(z, 2))
+    merged = (jnp.logical_or(merged, ahead == 3 + 2 * rem(z, 2)), merged)
     for rel in range(4):
-        gi_v[:, pl.ds(pl.multiple_of(mate(rel) * 128, 128), 128)] = Ff[0, rel] + Ff[1, rel]
+        cols = pl.ds(pl.multiple_of(mate(rel) * 128, 128), 128)
+        if rel > 0:
+            piece(0, rel)
+        if rel > 1:
+            piece(1, rel)
+            gi_v[:, cols] = Ff[0, rel] + Ff[1, rel]
+        else:
+
+            @pl.when(merged[rel])
+            def _(rel=rel, cols=cols):
+                gi_v[:, cols] = Ff[0, rel]
+
+            @pl.when(jnp.logical_not(merged[rel]))
+            def _(rel=rel, cols=cols):
+                piece(1, rel)
+                gi_v[:, cols] = Ff[0, rel] + Ff[1, rel]
+
     out_gi = pltpu.make_async_copy(gi_v, o_gi, loc.at[0])
     out_gi.start()
 
+    z_step(4)
     for rel in (1, 2, 3):
         r_copy(rel).wait_recv()
     for h in (0, 1):
@@ -480,26 +584,20 @@
         outs.append(pltpu.make_async_copy(src, dst, loc.at[i + 1]))
         outs[-1].start()
 
-    for j in (1, 2, 3, 4):
-        for way in (0, 1):
-            for h in (0, 1):
-                if j < 4 or h == FIRST[way]:
-                    w_copy(way, j, h).wait_send()
-                    m_copy(way, j, h).wait_send()
-    for h in (0, 1):
-        for rel in (1, 2, 3):
-            g_copy(rel, h).wait_send()
-    for rel in (1, 2, 3):
-        b_copy(rel).wait_send()
-        sq_copy(rel).wait_send()
-        nq_copy(rel).wait_send()
-        ma_copy(rel, fm).wait_send()
-        i_copy(rel).wait_send()
-        r_copy(rel).wait_send()
-    for j in range(4):
-        for way in (0, 1):
-            Tree(Z, ZR, COLS, z_s, z_r).copy(way, j).wait_send()
-            Tree(Y, YR, RANK, y_s, y_r).copy(way, j).wait_send()
+    def sent(ref, sem):
+        remote(ref, ref, sem, sem, zl).wait_send()
+
+    for way in (0, 1):
+        sent(Ws.at[pl.ds(0, 448)], w_s.at[way])
+        sent(Ms.at[pl.ds(0, 224)], m_s.at[way])
+    sent(Gs.at[pl.ds(0, 3)], g_s.at[0])
+    z_tree.close()
+    i_tree.close()
+    three = pl.ds(1, 3)
+    rows48 = pl.ds(0, 48)
+    for kind, ref in enumerate((Bs.at[three], Sq.at[three], Nq.at[three], Ms.at[rows48], I64.at[three], RT.at[rows48])):
+        sent(ref, k_s.at[kind])
+    sent(Y.at[pl.ds(0, 3)], ix_s.at[0])
     run(drain, (5, 3, 0, 1))
     for cp in outs:
         cp.wait()
@@ -529,22 +627,23 @@
             pltpu.VMEM((TOK, RANK), BF16),
             pltpu.VMEM((DROWS, RANK), BF16),
             pltpu.VMEM((4, TOK, COLS), BF16),
-            pltpu.VMEM((8, DROWS, COLS), BF16),
+            pltpu.VMEM((8 * DROWS, COLS), BF16),
             pltpu.VMEM((8, 4, TOK, DROWS), F32),
             pltpu.VMEM((8, 4, DROWS, DROWS), F32),
             pltpu.VMEM((8, 4, DROWS, DROWS), F32),
+            pltpu.VMEM((3, 2, TOK, DROWS), F32),
             pltpu.VMEM((2, 4, TOK, DROWS), F32),
             pltpu.VMEM((8, 4, 16, TOK), BF16),
             pltpu.VMEM((4, 8, 16, TOK), BF16),
             pltpu.VMEM((8, 4, 16, DROWS), BF16),
             pltpu.VMEM((4, 8, 16, DROWS), BF16),
-            pltpu.VMEM((4, DROWS, RANK), BF16),
+            pltpu.VMEM((4, DROWS, 128), BF16),
             pltpu.VMEM((RANK, HALF), F32),
             pltpu.VMEM((8, 16, COLS), F32),
             pltpu.VMEM((2, 4, 16, COLS), F32),
-            pltpu.VMEM((8, 16, RANK), F32),
-            pltpu.VMEM((2, 4, 16, RANK), F32),
-            pltpu.VMEM((4, 16, RANK), F32),
+            pltpu.VMEM((8, 16, 128), F32),
+            pltpu.VMEM((2, 4, 16, 128), F32),
+            pltpu.VMEM((4, 4, 16, 128), F32),
             pltpu.VMEM((64, HALF), F32),
             pltpu.VMEM((2, 2, 16, HALF), F32),
             pltpu.VMEM((TOK, RANK), F32),
@@ -552,22 +651,26 @@
             pltpu.VMEM((ROWS, COLS), F32),
             pltpu.VMEM((ROWS, COLS), F32),
             dma((6,)),
+            dma((1,)),
             dma((3, 2)),
-            dma((3, 2)),
+            dma((6,)),
             dma((6, 3)),
-            dma((6, 3)),
+            dma((2,)),
             dma((2, 4, 2)),
+            dma((2,)),
             dma((2, 4, 2)),
-            dma((2, 4, 2)),
-            dma((2, 4, 2)),
+            dma((2,)),
             dma((2, 4)),
+            dma((2,)),
             dma((2, 4)),
-            dma((2, 4)),
-            dma((2, 4)),
+            dma((1,)),
+            dma((3,)),
             dma((8,)),
             dma((8,)),
             dma((8, 4)),
             dma((8, 4)),
+            dma((3, 2)),
+            dma((3, 2)),
             dma((2, 4)),
             dma((2, 4)),
         ],

time: 89.9 us -> 84.1 us (0.935)
  Pallas kernels: 89.2 us -> 83.4 us
    pallas_call x1, Pallas kernels: 87.2 us -> 81.4 us  [per_device(): pl.pallas_call(kernel, out_shape=(jax.ShapeDtypeStruct((TOK, RANK), F32),...]
where the time goes in v3:
time: 84.1 us; the launch traced here: 84 us
  Pallas kernels  83.4 us (99%)
    pallas_call x1, Pallas kernels, per_device(): pl.pallas_call(kernel, out_shape=(jax.ShapeDtypeStruct((TOK, RANK), F32),...  81.4 us
    pallas_call x1, Pallas kernels, per_device(): pl.pallas_call(hand_over, out_shape=(jax.ShapeDtypeStruct((TOK, RANK), F3...  2.01 us

profile of v3, /device:TPU:1, one launch (start us, length us, event | category | flops | bytes accessed | tf_op | source)
XLA Modules:
  0.0 84.0 jit_solution(9343245284092567147)
XLA Ops:
  0.6 81.4 %shard_map.102 = (f32[256,512]{1,0:T(8,128)}, f32[16,1792]{1,0:T(8,128)}, f32[16,1792]{1,0:T(8,128)}, f32[16,1792]{1,0:T(8,128)}) custom-call(bf16[256,1792]{1,0:T(8,128)(2,1)} %go.1, bf16[128,1792]{1,0:T(8,128)(2,1)} %w.1, bf16[256,512]{1,0:T(8,128)(2,1)} %sv_h.1, f32[16,1792]{1,0:T(8,128)} %fm.1, f32[16,1792]{1,0:T(8,128)} %sm.1, bf16[128,512]{1,0:T(8,128)(2,1)} %ba.1, ...), custom_call_target="tpu_custom_call" | custom-call | tf_op jit(solution)/shard_map/pallas_call | solution.py:621
  82.0 2.0 %shard_map.103 = (f32[256,512]{1,0:T(8,128)}, f32[16,1792]{1,0:T(8,128)}, f32[16,1792]{1,0:T(8,128)}, f32[16,1792]{1,0:T(8,128)}) custom-call(f32[256,512]{1,0:T(8,128)} %get-tuple-element.8.a, f32[16,1792]{1,0:T(8,128)} %get-tuple-element.9.b, f32[16,1792]{1,0:T(8,128)} %get-tuple-element.10.c, f32[16,1792]{1,0:T(8,128)} %get-tuple-element.11.d), custom_call_target="tpu_custom_call" | custom-call | tf_op jit(solution)/shard_map/pallas_call | solution.py:681

commit v4 on v3

--- a/solution.py
+++ b/solution.py
@@ -130,9 +130,12 @@
     def ix_copy(step):
         return remote(Y.at[z], I64.at[k, x], ix_s.at[0], ix_r.at[step - 1], (s, rem(x + step, 4) * 2 + yh))
 
-    def r_copy(rel):
+    PARTS = (pl.ds(0, 512), pl.ds(512, HALF - 512))
+
+    def r_copy(rel, part):
+        cols = PARTS[part]
         rows = pl.ds(pl.multiple_of(mate(rel) * 16, 16), 16)
-        return remote(RT.at[rows], Rr.at[c, yl], k_s.at[5], k_r.at[5, rel - 1], group_dev(rel))
+        return remote(RT.at[rows, cols], Rr.at[c, yl, :, cols], k_s.at[5], k_r.at[5 + part, rel - 1], group_dev(rel))
 
     def z_block(way, j):
         dist = 4 - j
@@ -532,9 +535,10 @@
 
     coef = jnp.concatenate([I64[:, i].reshape(64, 128) for i in range(4)], axis=1)
     coef = jnp.where(c == 0, coef, coef * coef)
-    RT[...] = jnp.dot(coef, Ms[...], precision=lax.Precision.HIGHEST, preferred_element_type=F32)
-    for rel in (1, 2, 3):
-        r_copy(rel).start()
+    for part, cols in enumerate(PARTS):
+        RT[:, cols] = jnp.dot(coef, Ms[:, cols], precision=lax.Precision.HIGHEST, preferred_element_type=F32)
+        for rel in (2, 3, 1):
+            r_copy(rel, part).start()
     run(stage4, E0)
     run(stage4, G0)
     run(stage4, F0)
@@ -569,7 +573,8 @@
 
     z_step(4)
     for rel in (1, 2, 3):
-        r_copy(rel).wait_recv()
+        r_copy(rel, 0).wait_recv()
+        r_copy(rel, 1).wait_recv()
     for h in (0, 1):
         cols = pl.ds(h * HALF, HALF)
         grad = Z[z, :, cols]
@@ -604,7 +609,8 @@
 
 
 def hand_over(a, b, c, d, oa, ob, oc, od, va, vb, vc, vd, sem):
-    triples = ((a, va, oa), (b, vb, ob), (c, vc, oc), (d, vd, od))
+    triples = [tuple(ref.at[pl.ds(i * 64, 64)] for ref in (a, va, oa)) for i in range(4)]
+    triples += [(b, vb, ob), (c, vc, oc), (d, vd, od)]
     for i, (src, mid, _) in enumerate(triples):
         pltpu.make_async_copy(src, mid, sem.at[0, i]).start()
     for i, (src, mid, dst) in enumerate(triples):
@@ -654,7 +660,7 @@
             dma((1,)),
             dma((3, 2)),
             dma((6,)),
-            dma((6, 3)),
+            dma((7, 3)),
             dma((2,)),
             dma((2, 4, 2)),
             dma((2,)),
@@ -683,7 +689,7 @@
         out_shape=(jax.ShapeDtypeStruct((TOK, RANK), F32), rank, rank, rank),
         in_specs=[hbm] * 4,
         out_specs=(hbm,) * 4,
-        scratch_shapes=[pltpu.VMEM((TOK, RANK), F32)] + [pltpu.VMEM((ROWS, COLS), F32)] * 3 + [dma((2, 4))],
+        scratch_shapes=[pltpu.VMEM((TOK, RANK), F32)] + [pltpu.VMEM((ROWS, COLS), F32)] * 3 + [dma((2, 7))],
     )(*results)
 
 

time: 84.1 us -> 83.9 us (level)
  no operation moved by 1% of the time
where the time goes in v4:
time: 83.9 us; the launch traced here: 83.8 us
  Pallas kernels  83.1 us (99%)
    pallas_call x1, Pallas kernels, per_device(): pl.pallas_call(kernel, out_shape=(jax.ShapeDtypeStruct((TOK, RANK), F32),...  81.1 us
    pallas_call x1, Pallas kernels, per_device(): pl.pallas_call(hand_over, out_shape=(jax.ShapeDtypeStruct((TOK, RANK), F3...  2 us

profile of v4, /device:TPU:1, one launch (start us, length us, event | category | flops | bytes accessed | tf_op | source)
XLA Modules:
  0.0 83.8 jit_solution(12737303591871417579)
XLA Ops:
  0.6 81.1 %shard_map.102 = (f32[256,512]{1,0:T(8,128)}, f32[16,1792]{1,0:T(8,128)}, f32[16,1792]{1,0:T(8,128)}, f32[16,1792]{1,0:T(8,128)}) custom-call(bf16[256,1792]{1,0:T(8,128)(2,1)} %go.1, bf16[128,1792]{1,0:T(8,128)(2,1)} %w.1, bf16[256,512]{1,0:T(8,128)(2,1)} %sv_h.1, f32[16,1792]{1,0:T(8,128)} %fm.1, f32[16,1792]{1,0:T(8,128)} %sm.1, bf16[128,512]{1,0:T(8,128)(2,1)} %ba.1, ...), custom_call_target="tpu_custom_call" | custom-call | tf_op jit(solution)/shard_map/pallas_call | solution.py:627
  81.8 2.0 %shard_map.103 = (f32[256,512]{1,0:T(8,128)}, f32[16,1792]{1,0:T(8,128)}, f32[16,1792]{1,0:T(8,128)}, f32[16,1792]{1,0:T(8,128)}) custom-call(f32[256,512]{1,0:T(8,128)} %get-tuple-element.8.a, f32[16,1792]{1,0:T(8,128)} %get-tuple-element.9.b, f32[16,1792]{1,0:T(8,128)} %get-tuple-element.10.c, f32[16,1792]{1,0:T(8,128)} %get-tuple-element.11.d), custom_call_target="tpu_custom_call" | custom-call | tf_op jit(solution)/shard_map/pallas_call | solution.py:687
